TPU v7x, 128 devices: a whole 4x4x4 slice. The times are simulated.
128 devices in a mesh: ep: 32 (over z, x, core), tp: 4 (over y).
Axes of the slice: x: 4, y: 4, z: 4, core: 2. Of those that a mesh axis runs over, the one named last changes fastest.
Arguments:
- resid: bfloat16 [8192, 1536], P('ep'), may hold values from -6 to 6
- context: bfloat16 [8192, 1536], P('ep', 'tp'), may hold values from -6 to 6
- w_out: bfloat16 [1536, 1536], P('tp'), may hold values from -0.15625 to 0.15625
- pre_gain: bfloat16 [1536], replicated, may hold values from 0.5 to 1.5
- final_gain: bfloat16 [1536], replicated, may hold values from 0.5 to 1.5
- w_router: bfloat16 [1536, 40], replicated, may hold values from -0.03491211 to 0.03491211
- expert_ids: int32 [8192, 8], P('ep'), may hold values from 0 to 39, all different within a row; in each aligned block of 256 rows (0 to 255, 256 to 511, ...) at most 80 rows name the same one
- slot_expert: int32 [64], replicated, may hold values from 0 to 39, as said below
- copy_pick: int32 [32, 40], P('ep'), may hold values from 0 to 7
- w_gate: bfloat16 [64, 1536, 512], P('ep', None, 'tp'), may hold values from -0.15625 to 0.15625
- w_up: bfloat16 [64, 1536, 512], P('ep', None, 'tp'), may hold values from -0.15625 to 0.15625
- w_down: bfloat16 [64, 512, 1536], P('ep', 'tp'), may hold values from -0.25 to 0.25
Outputs:
- layer_out: bfloat16 [8192, 1536], P('ep')
Inputs may be any that keep to these rules, and one draw needn't show every extreme that they name: `expert_ids`: each row names 8 different experts; among the rows of one index of ep no expert is named by more than 80 rows, a bound that some block reaches of them. `slot_expert`: every expert is held by at least one slot.
All inputs are finite; a program needn't handle non-finite values.
Results may differ from a plain program's by a relative error of at most 0.012.
Values may be sent and summed in bfloat16 or wider, within the bound.
A program may use at most 128 MiB of HBM per device.

v0:
```python
import jax
import jax.numpy as jnp
from jax import lax
from jax.sharding import PartitionSpec as P

CAP = 80


EPSILON = 1e-06


def shortened(value):

    def short(part):
        return part.astype(jnp.bfloat16) if part.dtype == jnp.float32 else part

    return jax.tree.map(short, value)


def rms_scaled(values, gain):
    mean_square = jnp.mean(values * values, axis=-1, keepdims=True)
    return values * lax.rsqrt(mean_square + EPSILON) * gain.astype(jnp.float32)


def slot_of_pick(slot_expert, copy_pick, experts):
    count = slot_expert.shape[0]
    order = jnp.arange(count, dtype=jnp.int32)
    same = slot_expert[:, None] == slot_expert[None, :]
    before = order[None, :] < order[:, None]
    rank = jnp.sum((same & before).astype(jnp.int32), axis=1)
    holds = slot_expert[None, :] == jnp.arange(experts, dtype=jnp.int32)[:, None]
    copies = jnp.sum(holds.astype(jnp.int32), axis=1)
    wanted = copy_pick % copies[None, :]
    match = holds[None, :, :] & (rank[None, None, :] == wanted[:, :, None])
    return jnp.sum(match.astype(jnp.int32) * order[None, None, :], axis=2)


def expert_rows(block, w_gate, w_up, w_down):
    depth, owners, held, width = block.shape
    results = []
    for number in range(held):
        rows_in = block[:, :, number, :].reshape(depth * owners, width)
        gate = jnp.dot(rows_in, w_gate[number], preferred_element_type=jnp.float32)
        upper = jnp.dot(rows_in, w_up[number], preferred_element_type=jnp.float32)
        hidden = (jax.nn.silu(gate) * upper).astype(jnp.bfloat16)
        output = jnp.dot(hidden, w_down[number], preferred_element_type=jnp.float32).astype(
            jnp.bfloat16
        )
        results.append(output.reshape(depth, owners, width))
    return jnp.stack(results, axis=2)


def local(
    resid,
    context,
    w_out,
    pre_gain,
    final_gain,
    w_router,
    expert_ids,
    slot_expert,
    copy_pick,
    w_gate,
    w_up,
    w_down,
):
    owners = lax.axis_size("ep")
    held = w_gate.shape[0]
    row_count, width = resid.shape
    choose = expert_ids.shape[1]
    experts = w_router.shape[1]
    attention = lax.psum(
        jnp.dot(context, w_out, preferred_element_type=jnp.float32).astype(jnp.bfloat16), "tp"
    ).astype(jnp.float32)
    middle = resid.astype(jnp.float32) + attention
    normed = rms_scaled(middle, pre_gain).astype(jnp.bfloat16)
    logits = jnp.dot(normed, w_router, preferred_element_type=jnp.float32)
    onehot = expert_ids[:, :, None] == jnp.arange(experts, dtype=jnp.int32)[None, None, :]
    chosen = jnp.sum(jnp.where(onehot, logits[:, None, :], 0.0), axis=2)
    raised = jnp.exp(chosen)
    weights = (raised / jnp.sum(raised, axis=1, keepdims=True)).astype(jnp.bfloat16)
    table = slot_of_pick(slot_expert, copy_pick, experts)[0]
    slot = jnp.sum(jnp.where(onehot, table[None, None, :], 0), axis=2).reshape(-1)
    flat_hot = onehot.reshape(row_count * choose, experts).astype(jnp.int32)
    earlier = jnp.cumsum(flat_hot, axis=0) - flat_hot
    position = jnp.sum(earlier * flat_hot, axis=1)
    target = slot // held
    local_slot = slot % held
    source_row = jnp.arange(row_count * choose, dtype=jnp.int32) // choose
    flat_index = (position * owners + target) * held + local_slot
    outbound = (
        jnp.zeros((CAP * owners * held, width), jnp.bfloat16).at[flat_index].set(normed[source_row])
    )
    outbound = outbound.reshape(CAP, owners, held, width)
    inbound = lax.all_to_all(outbound, "ep", split_axis=1, concat_axis=1, tiled=True)
    step_rows = 16

    def block_term(number):
        block = lax.dynamic_slice_in_dim(inbound, number * step_rows, step_rows, 0)
        return expert_rows(block, w_gate, w_up, w_down)

    partial_value = lax.map(block_term, jnp.arange(CAP // step_rows, dtype=jnp.int32)).reshape(
        inbound.shape
    )
    returned = lax.all_to_all(
        shortened(partial_value), "ep", split_axis=1, concat_axis=1, tiled=True
    ).astype(partial_value.dtype)
    picked = returned.reshape(-1, width)[flat_index].reshape(row_count, choose, width)
    mixture_lane = jnp.einsum("rk,rkd->rd", weights, picked, preferred_element_type=jnp.float32)
    mixture = lax.psum(mixture_lane.astype(jnp.bfloat16), "tp").astype(jnp.float32)
    return rms_scaled(middle + mixture, final_gain).astype(jnp.bfloat16)


def solution(mesh):
    return jax.shard_map(
        local,
        mesh=mesh,
        in_specs=(
            P("ep", None),
            P("ep", "tp"),
            P("tp", None),
            P(),
            P(),
            P(),
            P("ep", None),
            P(),
            P("ep", None),
            P("ep", None, "tp"),
            P("ep", None, "tp"),
            P("ep", "tp", None),
        ),
        out_specs=P("ep", None),
        check_vma=False,
    )
```

profile of v0, /device:TPU:0, one launch (start us, length us, event | category | flops | bytes accessed | tf_op | source)
XLA Modules:
  0.0 862.8 jit_solution(4662891547152747699)
XLA Ops:
  10.9 11.3 %reduce-window.6 = s32[40,16,128]{2,1,0:T(8,128)S(1)} reduce-window(s32[40,16,128]{2,1,0:T(8,128)S(1)} %fusion.42, s32[]{:T(128)} %constant.75.clone.1), window={size=1x1x128 pad=0_0x0_0x127_0}, to_apply=%region_4.5 | reduce-window | flops 10403840 | bytes 655364 | tf_op jit(solution)/shard_map/reduce-window
  24.1 33.2 %all-reduce.3.cloned.1.call-done = bf16[256,1536]{1,0:T(8,128)(2,1)} async-done(((bf16[256,1536]{1,0:T(8,128)(2,1)}), bf16[256,1536]{1,0:T(8,128)(2,1)}) %all-reduce.3.cloned.1.call-update) | async-done | bytes 786448 | tf_op jit(solution)/shard_map/psum | solution.py:72
  59.2 40.0 %scatter_custom_fusion = bf16[5120,1536]{1,0:T(8,128)(2,1)} fusion(s32[2048]{0:T(1024)S(1)} %bitcast.118, bf16[]{:T(256)} %constant.76.clone.1, bf16[256,1536]{1,0:T(8,128)(2,1)S(1)} %multiply_convert_fusion.1, s32[2048]{0:T(1024)S(1)} %broadcast_clamp_fusion.1), kind=kCustom, calls=%fused_computation.41 | custom fusion | bytes 15728642 | tf_op jit(solution)/shard_map/scatter | solution.py:92
  99.2 30.9 %reshape.353 = bf16[80,32,2,1536]{3,2,1,0:T(2,128)(2,1)} reshape(bf16[5120,1536]{1,0:T(8,128)(2,1)} %scatter_custom_fusion) | data formatting | bytes 31457280 | tf_op jit(solution)/shard_map/reshape | solution.py:94
  130.1 17.4 %copy.48 = bf16[80,32,2,1536]{3,2,0,1:T(2,128)(2,1)} copy(bf16[80,32,2,1536]{3,2,1,0:T(2,128)(2,1)} %reshape.353) | data formatting | bytes 31457280 | tf_op jit(solution)/shard_map/reshape | solution.py:94
  147.5 7.5 all-to-all-start
  155.0 199.8 %all-to-all-done = bf16[80,32,2,1536]{3,2,0,1:T(2,128)(2,1)} async-done(((bf16[80,32,2,1536]{3,2,0,1:T(2,128)(2,1)}), bf16[80,32,2,1536]{3,2,0,1:T(2,128)(2,1)}, u32[]{:S(2)}, u32[]{:S(2)}) %all-to-all-start) | async-done | bytes 15728672 | tf_op jit(solution)/shard_map/all_to_all | solution.py:95
  354.8 150.0 %while.10 = (s32[]{:T(128)}, bf16[5,16,32,2,1536]{4,2,3,1,0:T(8,128)(2,1)}, s32[5]{0:T(128)S(1)}, bf16[80,32,2,1536]{3,2,0,1:T(2,128)(2,1)}, bf16[2,1536,128]{2,...) while((s32[]{:T(128)}, ...), condition=%wide.region_13.14_spmd, body=%wide.region_12.13_spmd.sunk | while | flops 1211891712 | bytes 38011144 | solution.py:102
  356.4 12.3 %constant_dynamic-slice_fusion.3 = (bf16[16,32,1,1536]{3,2,0,1:T(2,128)(2,1)}, bf16[16,32,1,1536]{3,2,0,1:T(2,128)(2,1)S(1)}) fusion(bf16[80,32,2,1536]{3,2,0,1:T(2,128)(2,1)} %get-tuple-element.154, s32[]{:T(128)S(6)} %select_n.127, s32[]{:T(128)S(6)} %add.180), kind=kLoop, calls=%fused_computation.37.clone.1 | loop fusion | bytes 6291464 | tf_op jit(solution)/shard_map/while/body/eval_jaxpr/slice | solution.py:42
  373.9 3.6 copy.71
  378.1 2.9 convolution_convert_fusion.6
  381.1 3.9 copy_dynamic-update-slice_fusion.2
  386.3 12.3 %constant_dynamic-slice_fusion.3 = (bf16[16,32,1,1536]{3,2,0,1:T(2,128)(2,1)}, bf16[16,32,1,1536]{3,2,0,1:T(2,128)(2,1)S(1)}) fusion(bf16[80,32,2,1536]{3,2,0,1:T(2,128)(2,1)} %get-tuple-element.154, s32[]{:T(128)S(6)} %select_n.127, s32[]{:T(128)S(6)} %add.180), kind=kLoop, calls=%fused_computation.37.clone.1 | loop fusion | bytes 6291464 | tf_op jit(solution)/shard_map/while/body/eval_jaxpr/slice | solution.py:42
  403.8 3.6 copy.71
  410.9 3.9 copy_dynamic-update-slice_fusion.2
  416.2 12.3 %constant_dynamic-slice_fusion.3 = (bf16[16,32,1,1536]{3,2,0,1:T(2,128)(2,1)}, bf16[16,32,1,1536]{3,2,0,1:T(2,128)(2,1)S(1)}) fusion(bf16[80,32,2,1536]{3,2,0,1:T(2,128)(2,1)} %get-tuple-element.154, s32[]{:T(128)S(6)} %select_n.127, s32[]{:T(128)S(6)} %add.180), kind=kLoop, calls=%fused_computation.37.clone.1 | loop fusion | bytes 6291464 | tf_op jit(solution)/shard_map/while/body/eval_jaxpr/slice | solution.py:42
  433.6 3.6 copy.71
  440.8 3.9 copy_dynamic-update-slice_fusion.2
  446.0 12.3 %constant_dynamic-slice_fusion.3 = (bf16[16,32,1,1536]{3,2,0,1:T(2,128)(2,1)}, bf16[16,32,1,1536]{3,2,0,1:T(2,128)(2,1)S(1)}) fusion(bf16[80,32,2,1536]{3,2,0,1:T(2,128)(2,1)} %get-tuple-element.154, s32[]{:T(128)S(6)} %select_n.127, s32[]{:T(128)S(6)} %add.180), kind=kLoop, calls=%fused_computation.37.clone.1 | loop fusion | bytes 6291464 | tf_op jit(solution)/shard_map/while/body/eval_jaxpr/slice | solution.py:42
  463.5 3.6 copy.71
  470.7 4.0 copy_dynamic-update-slice_fusion.2
  476.0 12.3 %constant_dynamic-slice_fusion.3 = (bf16[16,32,1,1536]{3,2,0,1:T(2,128)(2,1)}, bf16[16,32,1,1536]{3,2,0,1:T(2,128)(2,1)S(1)}) fusion(bf16[80,32,2,1536]{3,2,0,1:T(2,128)(2,1)} %get-tuple-element.154, s32[]{:T(128)S(6)} %select_n.127, s32[]{:T(128)S(6)} %add.180), kind=kLoop, calls=%fused_computation.37.clone.1 | loop fusion | bytes 6291464 | tf_op jit(solution)/shard_map/while/body/eval_jaxpr/slice | solution.py:42
  493.5 3.6 copy.71
  500.6 4.0 copy_dynamic-update-slice_fusion.2
  504.8 29.5 %copy.51 = bf16[80,32,2,1536]{3,2,0,1:T(2,128)(2,1)} copy(bf16[80,32,2,1536]{3,1,2,0:T(8,128)(2,1)} %bitcast.113) | data formatting | bytes 31457280 | tf_op jit(solution)/shard_map/reshape | solution.py:102
  534.4 5.3 all-to-all-start.1
  540.3 199.2 %all-to-all-done.1 = bf16[80,32,2,1536]{3,2,0,1:T(2,128)(2,1)} async-done(((bf16[80,32,2,1536]{3,2,0,1:T(2,128)(2,1)}), bf16[80,32,2,1536]{3,2,0,1:T(2,128)(2,1)}, u32[]{:S(2)}, u32[]{:S(2)}) %all-to-all-start.1) | async-done | bytes 15728672 | tf_op jit(solution)/shard_map/all_to_all | solution.py:105
  739.5 13.8 %copy.52 = bf16[80,32,2,1536]{3,2,1,0:T(2,128)(2,1)} copy(bf16[80,32,2,1536]{3,2,0,1:T(2,128)(2,1)} %all-to-all-done.1) | data formatting | bytes 31457280 | tf_op jit(solution)/shard_map/all_to_all | solution.py:105
  753.3 32.1 %reshape.355 = bf16[5120,1536]{1,0:T(8,128)(2,1)} reshape(bf16[80,32,2,1536]{3,2,1,0:T(2,128)(2,1)} %copy.52) | data formatting | bytes 31457280 | tf_op jit(solution)/shard_map/reshape | solution.py:108
  785.4 20.8 %gather_fusion = bf16[2048,1536]{1,0:T(8,128)(2,1)} fusion(bf16[5120,1536]{1,0:T(8,128)(2,1)} %reshape.355, s32[2048]{0:T(1024)S(1)} %broadcast_clamp_fusion), kind=kCustom, calls=%fused_computation.1 | custom fusion | bytes 12591104 | tf_op jit(solution)/shard_map/gather | solution.py:108
  806.2 4.6 fusion.36
  811.8 40.8 %all-reduce.5.cloned.1.call-done = bf16[256,1536]{1,0:T(8,128)(2,1)} async-done(((bf16[256,1536]{1,0:T(8,128)(2,1)}), bf16[256,1536]{1,0:T(8,128)(2,1)}) %all-reduce.5.cloned.1.call-update) | async-done | bytes 786448 | tf_op jit(solution)/shard_map/psum | solution.py:110
  (125 shorter events, 56.2 us)
Async XLA Ops:
  6.5 1.3 copy-start
  6.5 3.7 copy-start.14
  6.5 4.0 copy-start.17
  6.5 4.3 copy-start.15
  6.5 50.7 %all-reduce.3.cloned.1.call-start = ((), (), s32[]{:S(2)}) async-start(), calls=%async_computation.2 | async-start | bytes 1572864 | tf_op jit(solution)/shard_map/psum | solution.py:72
  10.6 12.7 %copy-start.18 = (s32[1,40]{1,0:T(1,128)S(1)}, s32[1,40]{1,0:T(1,128)}, u32[]{:S(2)}) copy-start(s32[1,40]{1,0:T(1,128)} %param.22) | copy-start | bytes 484
  10.9 46.4 %copy-start.6 = (bf16[256,1536]{1,0:T(8,128)(2,1)S(1)}, bf16[256,1536]{1,0:T(8,128)(2,1)}, u32[]{:S(2)}) copy-start(bf16[256,1536]{1,0:T(8,128)(2,1)} %param.14) | copy-start | bytes 2359300
  57.3 1.6 copy-start.8
  59.2 40.0 %copy-start.10 = (bf16[256,1536]{1,0:T(8,128)(2,1)}, bf16[256,1536]{1,0:T(8,128)(2,1)S(1)}, u32[]{:S(2)}) copy-start(bf16[256,1536]{1,0:T(8,128)(2,1)S(1)} %multiply_convert_fusion.1) | copy-start | bytes 2359300
  147.5 207.3 %copy-start.2 = (bf16[2,1536,128]{2,1,0:T(8,128)(2,1)S(1)}, bf16[2,1536,128]{2,1,0:T(8,128)(2,1)}, u32[]{:S(2)}) copy-start(bf16[2,1536,128]{2,1,0:T(8,128)(2,1)} %param.24) | copy-start | bytes 2359300
  147.5 207.3 %copy-start.3 = (bf16[2,128,1536]{2,1,0:T(8,128)(2,1)S(1)}, bf16[2,128,1536]{2,1,0:T(8,128)(2,1)}, u32[]{:S(2)}) copy-start(bf16[2,128,1536]{2,1,0:T(8,128)(2,1)} %param.25) | copy-start | bytes 2359300
  147.5 207.3 %all-to-all-start = ((bf16[80,32,2,1536]{3,2,0,1:T(2,128)(2,1)}), bf16[80,32,2,1536]{3,2,0,1:T(2,128)(2,1)}, u32[]{:S(2)}, u32[]{:S(2)}) async-start(bf16[80,32,2,1536]{3,2,0,1:T(2,128)(2,1)} %copy.48), calls=%async_computation | async-start | bytes 31457280 | tf_op jit(solution)/shard_map/all_to_all | solution.py:95
  368.7 1.7 copy-start.4
  373.9 3.6 copy-start.5
  398.6 1.7 copy-start.4
  403.7 3.6 copy-start.5
  428.5 1.7 copy-start.4
  433.6 3.6 copy-start.5
  458.3 1.7 copy-start.4
  463.5 3.6 copy-start.5
  488.3 1.7 copy-start.4
  493.5 3.6 copy-start.5
  534.3 5.3 copy-start.11
  534.4 5.3 copy-start.13
  534.4 205.2 %all-to-all-start.1 = ((bf16[80,32,2,1536]{3,2,0,1:T(2,128)(2,1)}), bf16[80,32,2,1536]{3,2,0,1:T(2,128)(2,1)}, u32[]{:S(2)}, u32[]{:S(2)}) async-start(bf16[80,32,2,1536]{3,2,0,1:T(2,128)(2,1)} %copy.51), calls=%async_computation.1 | async-start | bytes 31457280 | tf_op jit(solution)/shard_map/all_to_all | solution.py:105
  539.6 312.9 %all-reduce.5.cloned.1.call-start = ((), (), s32[]{:S(2)}) async-start(), calls=%async_computation.3 | async-start | bytes 1572864 | tf_op jit(solution)/shard_map/psum | solution.py:110
  810.7 1.0 copy-start.16
  810.7 41.8 %copy-start.7 = (bf16[256,1536]{1,0:T(8,128)(2,1)S(1)}, bf16[256,1536]{1,0:T(8,128)(2,1)}, u32[]{:S(2)}) copy-start(bf16[256,1536]{1,0:T(8,128)(2,1)} %param.14) | copy-start | bytes 2359300
  810.7 41.8 %copy-start.9 = (bf16[256,1536]{1,0:T(8,128)(2,1)S(1)}, bf16[256,1536]{1,0:T(8,128)(2,1)}, u32[]{:S(2)}) copy-start(bf16[256,1536]{1,0:T(8,128)(2,1)} %all-reduce.3.cloned.1.call-done) | copy-start | bytes 2359300
  852.6 1.7 copy-start.12
  854.2 1.3 copy-start.1
Sparse Core Ops, SparseCore 0:
  10.3 46.9 all-reduce.2
  811.9 40.6 all-reduce.4
where the time goes:
time: 874 us; the launch traced here: 863 us
  waiting for transfers between devices  473 us (54%)
  local copies, waits for them, and re-layouts  279 us (32%)
  matrix products  42.2 us (5%)
  other arithmetic  37.1 us (4%)
  between operations  14.2 us (2%)
  starting transfers between devices  12.8 us (1%)
    all_to_all x1, waiting for transfers between devices, local(): lax.all_to_all(outbound, 'ep', split_axis=1, concat_axis=1, tiled=True)  200 us
    all_to_all x1, waiting for transfers between devices, local(): lax.all_to_all(shortened(partial_value), 'ep', split_axis=1, concat_axis=...  199 us
    slice x5, local copies, waits for them, and re-layouts, expert_rows(): rows_in = block[:, :, number, :].reshape(depth * owners, width)  61.4 us
    reshape x2, local copies, waits for them, and re-layouts, local(): outbound = outbound.reshape(CAP, owners, held, width)  48.3 us
    psum x1, waiting for transfers between devices, local(): lax.psum(mixture_lane.astype(jnp.bfloat16), 'tp').astype(jnp.float32)  40.8 us
    scatter x1, local copies, waits for them, and re-layouts, local(): jnp.zeros((CAP * owners * held, width), jnp.bfloat16).at[flat_index]  40 us
    psum x1, waiting for transfers between devices, local(): lax.psum(jnp.dot(context, w_out, preferred_element_type=jnp.float32).asty...  33.2 us
    reshape x1, local copies, waits for them, and re-layouts, local(): returned.reshape(-1, width)[flat_index].reshape(row_count, choose, width)  32.1 us
  transfers between devices with their start and end apart: 4, of which 4 were waited for; matrix products, arithmetic and copies ran while one was open for 2% of the time, Pallas kernels for 0%

commit v1 on v0

v1 whole, which is shorter than its diff:
```python
import functools

import jax
import jax.numpy as jnp
from jax import lax
from jax.experimental import pallas as pl
from jax.experimental.pallas import tpu as pltpu
from jax.sharding import PartitionSpec as P

EPSILON = 1e-06
MESH = pl.DeviceIdType.MESH
F32 = jnp.float32
BF16 = jnp.bfloat16

D = 1536
QR = 64
HR = 128
XW = D + 128
GROUP = 4 * HR
EXPERTS = 40
SLOTS = 64


def ds(start, size, align=None):
    return pl.ds(pl.multiple_of(start, align or size), size)


def slot_choice(slot_expert, copy_pick):
    expert = lax.broadcasted_iota(jnp.int32, (EXPERTS, SLOTS), 0)
    holds = (slot_expert == expert).astype(F32)
    before = lax.broadcasted_iota(jnp.int32, (SLOTS, SLOTS), 0) < lax.broadcasted_iota(
        jnp.int32, (SLOTS, SLOTS), 1
    )
    rank = jnp.dot(
        holds.astype(BF16), before.astype(F32).astype(BF16), preferred_element_type=F32
    )
    copies = jnp.sum(holds, axis=1, keepdims=True)
    square = (EXPERTS, EXPERTS)
    diagonal = lax.broadcasted_iota(jnp.int32, square, 0) == lax.broadcasted_iota(
        jnp.int32, square, 1
    )
    pick = jnp.sum(
        jnp.where(diagonal, copy_pick.astype(F32), 0.0), axis=1, keepdims=True
    )
    wanted = pick - copies * jnp.floor((pick + 0.5) / copies)
    return jnp.where(jnp.abs(rank - wanted) < 0.5, holds, 0.0)


def kernel(
    resid,
    context,
    w_out,
    pre_gain,
    final_gain,
    w_router,
    expert_ids,
    slot_expert,
    copy_pick,
    w_gate,
    w_up,
    w_down,
    out,
    att_send,
    att_recv,
    middle,
    xall,
    wgu,
    wd,
    hid,
    yo,
    yr,
    ys,
    bhalf,
    bfull,
    z,
    ahalf,
    afull,
    psend,
    precv,
    result,
    send_sem,
    recv_sem,
    local_sem,
):
    ep = lax.axis_index("ep")
    t = lax.axis_index("tp")
    c = ep % 2
    xx = (ep // 2) % 4
    zz = ep // 8
    a = zz * (1 - c) + xx * c
    b = xx * (1 - c) + zz * c
    stride_a = 8 - 6 * c
    stride_b = 2 + 6 * c

    def along(da, db):
        return (((a + da) % 4) * stride_a + ((b + db) % 4) * stride_b + c, t)

    core = (ep + 1 - 2 * c, t)

    def lane(dt):
        return (ep, (t + dt) % 4)

    def pos(da, db):
        return c * 16 + ((b + db) % 4) * 4 + (a + da) % 4

    def group_own(db):
        return c * 4 + (b + db) % 4

    def group_core(db):
        return (1 - c) * 4 + (a + db) % 4

    counter = [0]
    sends = []

    def send(src, dst, device):
        i = counter[0]
        counter[0] += 1
        copy = pltpu.make_async_remote_copy(
            src_ref=src,
            dst_ref=dst,
            send_sem=send_sem.at[i],
            recv_sem=recv_sem.at[i],
            device_id=device,
            device_id_type=MESH,
        )
        copy.start()
        sends.append(copy)
        return i

    def arrived(i, ref):
        pltpu.make_async_remote_copy(
            src_ref=ref,
            dst_ref=ref,
            send_sem=send_sem.at[i],
            recv_sem=recv_sem.at[i],
            device_id=core,
            device_id_type=MESH,
        ).wait_recv()

    barrier = pltpu.get_barrier_semaphore()
    partners = [core, lane(1), lane(2), lane(3)]
    partners += [along(1, 0), along(3, 0), along(0, 1), along(0, 3)]
    for partner in partners:
        pl.semaphore_signal(barrier, inc=1, device_id=partner, device_id_type=MESH)

    local = []

    def fetch(src, dst):
        copy = pltpu.make_async_copy(src, dst, local_sem.at[len(local)])
        copy.start()
        local.append(copy)

    for s in range(2):
        fetch(w_gate.at[s], wgu.at[:, pl.ds(s * 512, 128)])
        fetch(w_up.at[s], wgu.at[:, pl.ds(s * 512 + 256, 128)])
        fetch(w_down.at[s], wd.at[pl.ds(s * 256, 128), :])

    def attention(dt):
        rows = context[ds(((t + dt) % 4) * QR, QR), :]
        return jnp.dot(rows, w_out[...], preferred_element_type=F32)

    att = {}
    for k, dt in enumerate((2, 1, 3)):
        att_send[k] = attention(dt).astype(BF16)
        if k == 0:
            pl.semaphore_wait(barrier, len(partners))
        att[k] = send(att_send.at[k], att_recv.at[k], lane(dt))
    own = attention(0)
    sel = slot_choice(slot_expert[...], copy_pick[...])
    for k in (1, 2, 0):
        arrived(att[k], att_recv.at[k])
        own = own + att_recv[k].astype(F32)
    mid = resid[ds(t * QR, QR), :].astype(F32) + own
    middle[...] = mid
    square = jnp.mean(mid * mid, axis=-1, keepdims=True)
    normed = (mid * lax.rsqrt(square + EPSILON) * pre_gain[...].astype(F32)).astype(BF16)
    logits = jnp.dot(normed, w_router[...], preferred_element_type=F32)
    ids = expert_ids[ds(t * QR, QR), :]
    expert = lax.broadcasted_iota(jnp.int32, (QR, EXPERTS), 1)
    named = ids[:, 0:1] == expert
    for k in range(1, 8):
        named = named | (ids[:, k : k + 1] == expert)
    raised = jnp.where(named, jnp.exp(jnp.where(named, logits, 0.0)), 0.0)
    weights = (raised / jnp.sum(raised, axis=1, keepdims=True)).astype(BF16)
    by_slot = jnp.dot(weights, sel.astype(BF16), preferred_element_type=F32).astype(BF16)

    mine = pos(0, 0)
    half = ds(mine * HR + (t // 2) * QR, QR)
    xall[half, pl.ds(0, D)] = normed
    xall[half, pl.ds(D, 128)] = jnp.concatenate(
        [by_slot, jnp.zeros((QR, 128 - SLOTS), BF16)], axis=1
    )
    i = send(xall.at[half, :], xall.at[half, :], lane(2))
    odd = t % 2
    wi = []
    for s, nb in ((0, lane(1 + 2 * odd)), (1, lane(3 - 2 * odd))):
        wi.append(
            (
                send(w_gate.at[s], wgu.at[:, pl.ds(s * 512 + 128, 128)], nb),
                wgu.at[:, pl.ds(s * 512 + 128, 128)],
            )
        )
        wi.append(
            (
                send(w_up.at[s], wgu.at[:, pl.ds(s * 512 + 384, 128)], nb),
                wgu.at[:, pl.ds(s * 512 + 384, 128)],
            )
        )
        wi.append(
            (
                send(w_down.at[s], wd.at[pl.ds(s * 256 + 128, 128), :], nb),
                wd.at[pl.ds(s * 256 + 128, 128), :],
            )
        )
    arrived(i, xall.at[ds(mine * HR + (1 - t // 2) * QR, QR), :])

    def block(p):
        return xall.at[ds(p * HR, HR), :]

    def part(p, h):
        return xall.at[ds(p * HR + h * QR, QR), :]

    def spread(p, device):
        return send(block(p), block(p), device)

    def spread_half(p, h, device):
        return send(part(p, h), part(p, h), device)

    def pos_core(da, db):
        return (1 - c) * 16 + ((a + db) % 4) * 4 + (b + da) % 4

    a_up, a_down, b_up, b_down = along(1, 0), along(3, 0), along(0, 1), along(0, 3)
    i_a0 = spread(mine, a_up)
    i_a1 = spread(mine, a_down)
    i_b0, i_b1, i_c, i_h0, i_h1 = {}, {}, {}, {}, {}

    def to_b(da):
        p = pos(da, 0)
        i_b0[da] = spread(p, b_up)
        i_b1[da] = spread(p, b_down)
        i_c[da, 0] = spread(p, core)

    def from_b(da):
        p = pos(da, 3)
        arrived(i_b0[da], block(p))
        i_h0[da] = spread_half(p, 0, b_up)
        i_c[da, 3] = spread(p, core)
        p = pos(da, 1)
        arrived(i_b1[da], block(p))
        i_h1[da] = spread_half(p, 1, b_down)
        i_c[da, 1] = spread(p, core)

    def far_b(da):
        p = pos(da, 2)
        arrived(i_h0[da], part(p, 0))
        arrived(i_h1[da], part(p, 1))
        i_c[da, 2] = spread(p, core)

    lanes = lax.broadcasted_iota(jnp.int32, (256, 128), 1)

    def hidden_of(group):
        @pl.loop(0, 2)
        def _(step):
            rows = ds(group * GROUP + step * 256, 256)
            by = xall[rows, pl.ds(D, 128)].astype(F32)
            for s in range(2):
                scale = jnp.sum(
                    jnp.where(lanes == ep * 2 + s, by, 0.0), axis=1, keepdims=True
                )
                both = jnp.dot(
                    xall[rows, pl.ds(0, D)],
                    wgu[:, pl.ds(s * 512, 512)],
                    preferred_element_type=F32,
                )
                gate, upper = both[:, :256], both[:, 256:]
                value = gate / (1.0 + jnp.exp(-gate)) * upper * scale
                hid[rows, pl.ds(s * 256, 256)] = value.astype(BF16)

    def core_group(db):
        for da in (0, 3, 1, 2):
            arrived(i_c[da, db], block(pos_core(da, db)))
        hidden_of(group_core(db))

    to_b(0)
    arrived(i_a0, block(pos(3, 0)))
    i_ah0 = spread_half(pos(3, 0), 0, a_up)
    to_b(3)
    arrived(i_a1, block(pos(1, 0)))
    i_ah1 = spread_half(pos(1, 0), 1, a_down)
    to_b(1)
    from_b(0)
    arrived(i_ah0, part(pos(2, 0), 0))
    arrived(i_ah1, part(pos(2, 0), 1))
    to_b(2)
    for copy in local:
        copy.wait()
    from_b(3)
    from_b(1)
    from_b(2)
    for j, ref in wi:
        arrived(j, ref)
    hidden_of(group_own(0))
    core_group(0)
    far_b(0)
    hidden_of(group_own(3))
    far_b(3)
    hidden_of(group_own(1))
    far_b(1)
    core_group(3)
    far_b(2)
    core_group(1)
    hidden_of(group_own(2))
    core_group(2)

    def down(group, dst):
        @pl.loop(0, 6)
        def _(step):
            rows = (step // 3) * 256
            columns = ds((step % 3) * 512, 512)
            value = jnp.dot(
                hid[ds(group * GROUP + rows, 256), :],
                wd[:, columns],
                preferred_element_type=F32,
            )
            dst[ds(rows, 256), columns] = value.astype(dst.dtype)

    def add_blocks(count, body):
        @pl.loop(0, count)
        def _(step):
            body(step)

    order = (2, 1, 3, 0)
    i_y = []
    for k, db in enumerate(order):
        down(group_core(db), yo.at[k])
        i_y.append(send(yo.at[k], yr.at[k], core))
    ranked = (2, 1, 3, 0)
    i_bh0, i_bh1 = {}, {}
    i_bf = {0: {}, 1: {}}

    def rows_of(da, h=None):
        at = ((a + da) % 4) * HR
        return ds(at, HR) if h is None else ds(at + h * QR, QR)

    for k, db in enumerate(order):
        down(group_own(db), ys.at[k])
        arrived(i_y[k], yr.at[k])
        if k == 0:
            for da in ranked:
                for h in range(2):
                    rows = rows_of(da, h)
                    ys[k, rows, :] = (ys[k, rows, :].astype(F32) + yr[k, rows, :].astype(F32)).astype(BF16)
                    if h == 0:
                        i_bh0[da] = send(ys.at[k, rows, :], bhalf.at[0, rows_of(da, 0), :], b_up)
                    else:
                        i_bh1[da] = send(ys.at[k, rows, :], bhalf.at[1, rows_of(da, 1), :], b_down)
        elif k < 3:
            h, ids_h, device = ((0, i_bh0, b_up), (1, i_bh1, b_down))[k - 1]
            for da in ranked:
                arrived(ids_h[da], bhalf.at[h, rows_of(da, h), :])
                rows = rows_of(da, h)
                ys[k, rows, :] = (
                    ys[k, rows, :].astype(F32)
                    + yr[k, rows, :].astype(F32)
                    + bhalf[h, rows, :].astype(F32)
                ).astype(BF16)
                rows = rows_of(da, 1 - h)
                ys[k, rows, :] = (ys[k, rows, :].astype(F32) + yr[k, rows, :].astype(F32)).astype(BF16)
                i_bf[h][da] = send(
                    ys.at[k, rows_of(da), :], bfull.at[h, rows_of(da), :], device
                )
    i_zh = {}
    for j, da in enumerate(ranked):
        rows = rows_of(da)
        for h in range(2):
            arrived(i_bf[h][da], bfull.at[h, rows, :])
        total = (
            ys[3, rows, :].astype(F32)
            + yr[3, rows, :].astype(F32)
            + bfull[0, rows, :].astype(F32)
            + bfull[1, rows, :].astype(F32)
        )
        if j == 0:
            z[j] = total.astype(BF16)
            i_zh[0] = send(z.at[j, pl.ds(0, QR), :], ahalf.at[0], a_up)
            i_zh[1] = send(z.at[j, pl.ds(QR, QR), :], ahalf.at[1], a_down)
        elif j < 3:
            h, device = ((0, a_up), (1, a_down))[j - 1]
            arrived(i_zh[h], ahalf.at[h])
            z[j, pl.ds((1 - h) * QR, QR), :] = total[(1 - h) * QR : (2 - h) * QR].astype(BF16)
            z[j, pl.ds(h * QR, QR), :] = (
                total[h * QR : (h + 1) * QR] + ahalf[h].astype(F32)
            ).astype(BF16)
            i_zh[2 + h] = send(z.at[j], afull.at[h], device)
        else:
            for h in range(2):
                arrived(i_zh[2 + h], afull.at[h])
            final = total + afull[0].astype(F32) + afull[1].astype(F32)

    upper_half = (t // 2).astype(F32)
    mine_rows = final[:QR] * (1.0 - upper_half) + final[QR:] * upper_half
    psend[...] = (final[:QR] * upper_half + final[QR:] * (1.0 - upper_half)).astype(BF16)
    i = send(psend, precv, lane(2))
    arrived(i, precv)
    value = middle[...] + (mine_rows + precv[...].astype(F32))
    square = jnp.mean(value * value, axis=-1, keepdims=True)
    value = value * lax.rsqrt(square + EPSILON) * final_gain[...].astype(F32)
    mine_out = ds(t * QR, QR)
    result[mine_out, :] = value.astype(BF16)
    i_out = [send(result.at[mine_out, :], result.at[mine_out, :], lane(dt)) for dt in (2, 1, 3)]
    for i, dt in zip(i_out, (2, 3, 1)):
        arrived(i, result.at[ds(((t + dt) % 4) * QR, QR), :])
    out[...] = result[...]
    for copy in sends:
        copy.wait_send()


COPIES = 128


def local(
    resid,
    context,
    w_out,
    pre_gain,
    final_gain,
    w_router,
    expert_ids,
    slot_expert,
    copy_pick,
    w_gate,
    w_up,
    w_down,
):
    vmem = pl.BlockSpec(memory_space=pltpu.VMEM)
    hbm = pl.BlockSpec(memory_space=pl.ANY)
    return pl.pallas_call(
        kernel,
        out_shape=jax.ShapeDtypeStruct((4 * QR, D), BF16),
        in_specs=[vmem] * 9 + [hbm] * 3,
        out_specs=vmem,
        scratch_shapes=[
            pltpu.VMEM((3, QR, D), BF16),
            pltpu.VMEM((3, QR, D), BF16),
            pltpu.VMEM((QR, D), F32),
            pltpu.VMEM((32 * HR, XW), BF16),
            pltpu.VMEM((D, 1024), BF16),
            pltpu.VMEM((512, D), BF16),
            pltpu.VMEM((32 * HR, 512), BF16),
            pltpu.VMEM((4, GROUP, D), BF16),
            pltpu.VMEM((4, GROUP, D), BF16),
            pltpu.VMEM((4, GROUP, D), BF16),
            pltpu.VMEM((2, GROUP, D), BF16),
            pltpu.VMEM((2, GROUP, D), BF16),
            pltpu.VMEM((3, HR, D), BF16),
            pltpu.VMEM((2, QR, D), BF16),
            pltpu.VMEM((2, HR, D), BF16),
            pltpu.VMEM((QR, D), BF16),
            pltpu.VMEM((QR, D), BF16),
            pltpu.VMEM((4 * QR, D), BF16),
            pltpu.SemaphoreType.DMA((COPIES,)),
            pltpu.SemaphoreType.DMA((COPIES,)),
            pltpu.SemaphoreType.DMA((6,)),
        ],
        compiler_params=pltpu.CompilerParams(
            collective_id=0, has_side_effects=True, vmem_limit_bytes=63 * 1024 * 1024
        ),
    )(
        resid,
        context,
        w_out,
        pre_gain[None, :],
        final_gain[None, :],
        w_router,
        expert_ids,
        slot_expert[None, :],
        copy_pick,
        w_gate,
        w_up,
        w_down,
    )


def solution(mesh):
    return jax.shard_map(
        local,
        mesh=mesh,
        in_specs=(
            P("ep", None),
            P("ep", "tp"),
            P("tp", None),
            P(),
            P(),
            P(),
            P("ep", None),
            P(),
            P("ep", None),
            P("ep", None, "tp"),
            P("ep", None, "tp"),
            P("ep", "tp", None),
        ),
        out_specs=P("ep", None),
        check_vma=False,
    )
```

time: 874 us -> 150 us (0.17); the launches traced: 863 us -> 149 us
  waiting for transfers between devices: 473 us -> 0 us
  local copies, waits for them, and re-layouts: 279 us -> 7.93 us
  Pallas kernels: 0 us -> 141 us
  matrix products: 42.2 us -> 0 us
  other arithmetic: 37.1 us -> 0 us
  between operations: 14.2 us -> 0.01 us
  starting transfers between devices: 12.8 us -> 0 us
    all_to_all x2 -> x0, waiting for transfers between devices: 399 us -> none  [the longest x1 200 us: local(): lax.all_to_all(outbound, 'ep', split_axis=1, concat_axis=1, tiled=True)]
    pallas_call x0 -> x1, Pallas kernels: none -> 141 us  [local(): pl.pallas_call(kernel, out_shape=jax.ShapeDtypeStruct((4 * QR, D), BF16),...]
    reshape x5 -> x0, local copies, waits for them, and re-layouts: 110 us -> none  [the longest x2 48.3 us: local(): outbound = outbound.reshape(CAP, owners, held, width)]
    psum x2 -> x0, waiting for transfers between devices: 74 us -> none  [the longest x1 40.8 us: local(): lax.psum(mixture_lane.astype(jnp.bfloat16), 'tp').astype(jnp.float32)]
    slice x6 -> x0, local copies, waits for them, and re-layouts: 61.6 us -> none  [the longest x5 61.4 us: expert_rows(): rows_in = block[:, :, number, :].reshape(depth * owners, width)]
    dot_general x23 -> x0, matrix products: 42.2 us -> none  [the longest x10 29.2 us: expert_rows(): jnp.dot(hidden, w_down[number], preferred_element_type=jnp.float32)]
    scatter x1 -> x0, local copies, waits for them, and re-layouts: 40 us -> none  [local(): jnp.zeros((CAP * owners * held, width), jnp.bfloat16).at[flat_index]]
    while x30 -> x0, local copies, waits for them, and re-layouts: 26.6 us -> none
  transfers between devices with their start and end apart: 4 -> 0, of which waited for: 4 -> 0; matrix products, arithmetic and copies ran while one was open for 2% -> 0% of each run, Pallas kernels for 0% -> 0%
where the time goes in v1:
time: 150 us; the launch traced here: 149 us
  Pallas kernels  141 us (94%)
  local copies, waits for them, and re-layouts  7.93 us (5%)
    pallas_call x1, Pallas kernels, local(): pl.pallas_call(kernel, out_shape=jax.ShapeDtypeStruct((4 * QR, D), BF16),...  141 us
    unnamed x3, local copies, waits for them, and re-layouts  5.36 us

profile of v1, /device:TPU:0, one launch (start us, length us, event | category | flops | bytes accessed | tf_op | source)
XLA Modules:
  0.0 148.7 jit_solution(18357494131028937733)
XLA Ops:
  0.0 1.3 broadcast_in_dim.9.pre_gain
  1.3 1.3 broadcast_in_dim.10.final_gain
  2.6 1.5 copy.14.expert_ids
  4.0 1.8 %copy.13.w_router = bf16[1536,40]{1,0:T(8,128)(2,1)} copy(bf16[1536,40]{0,1:T(8,128)(2,1)} %param.17) | data formatting | bytes 245760 | tf_op args[5]
  5.9 140.7 %shard_map.118 = bf16[256,1536]{1,0:T(8,128)(2,1)} custom-call(bf16[256,1536]{1,0:T(8,128)(2,1)} %resid.1, bf16[256,384]{1,0:T(8,128)(2,1)} %context.1, bf16[384,1536]{1,0:T(8,128)(2,1)} %w_out.1, bf16[1,1536]{1,0:T(2,128)(2,1)} %broadcast_in_dim.9.pre_gain, bf16[1,1536]{1,0:T(2,128)(2,1)} %broadcast_in_dim.10.final_gain, bf16[1536,40]{1,0:T(8,128)(2,1)} %copy.13.w_router, ...), custom_call_target="tpu_custom_call" | custom-call | tf_op jit(solution)/shard_map/pallas_call | solution.py:437
  146.6 2.1 %copy.16 = bf16[256,1536]{1,0:T(8,128)(2,1)} copy(bf16[256,1536]{1,0:T(8,128)(2,1)} %shard_map.118) | data formatting | bytes 1572864

commit v2 on v1

v2 whole, which is shorter than its diff:
```python
import functools

import jax
import jax.numpy as jnp
from jax import lax
from jax.experimental import pallas as pl
from jax.experimental.pallas import tpu as pltpu
from jax.sharding import PartitionSpec as P

EPSILON = 1e-06
MESH = pl.DeviceIdType.MESH
F32 = jnp.float32
BF16 = jnp.bfloat16

D = 1536
QR = 64
SR = QR // 2
XW = D + 128
GROUP = 4 * QR
EXPERTS = 40
SLOTS = 64


def ds(start, size, align=None):
    return pl.ds(pl.multiple_of(start, align or size), size)


def slot_choice(slot_expert, copy_pick):
    expert = lax.broadcasted_iota(jnp.int32, (EXPERTS, SLOTS), 0)
    holds = (slot_expert == expert).astype(F32)
    before = lax.broadcasted_iota(jnp.int32, (SLOTS, SLOTS), 0) < lax.broadcasted_iota(
        jnp.int32, (SLOTS, SLOTS), 1
    )
    rank = jnp.dot(
        holds.astype(BF16), before.astype(F32).astype(BF16), preferred_element_type=F32
    )
    copies = jnp.sum(holds, axis=1, keepdims=True)
    square = (EXPERTS, EXPERTS)
    diagonal = lax.broadcasted_iota(jnp.int32, square, 0) == lax.broadcasted_iota(
        jnp.int32, square, 1
    )
    pick = jnp.sum(
        jnp.where(diagonal, copy_pick.astype(F32), 0.0), axis=1, keepdims=True
    )
    wanted = pick - copies * jnp.floor((pick + 0.5) / copies)
    return jnp.where(jnp.abs(rank - wanted) < 0.5, holds, 0.0)


def kernel(
    resid,
    context,
    w_out,
    pre_gain,
    final_gain,
    w_router,
    expert_ids,
    slot_expert,
    copy_pick,
    w_gate,
    w_up,
    w_down,
    out,
    att_send,
    att_half,
    att_full,
    middle,
    relay,
    xall,
    wgu,
    wd,
    hid,
    yo,
    yr,
    ys,
    bhalf,
    bfull,
    z,
    ahalf,
    afull,
    psend,
    precv,
    send_sem,
    recv_sem,
    local_sem,
):
    ep = lax.axis_index("ep")
    t = lax.axis_index("tp")
    c = ep % 2
    xx = (ep // 2) % 4
    zz = ep // 8
    a = zz * (1 - c) + xx * c
    b = xx * (1 - c) + zz * c
    stride_a = 8 - 6 * c
    stride_b = 2 + 6 * c
    quarter = (t // 2, 1 - t // 2)

    def along(da, db):
        return (((a + da) % 4) * stride_a + ((b + db) % 4) * stride_b + c, t)

    core = (ep + 1 - 2 * c, t)
    a_up, a_down, b_up, b_down = along(1, 0), along(3, 0), along(0, 1), along(0, 3)

    def lane(dt):
        return (ep, (t + dt) % 4)

    counter = [0]
    sends = []

    def send(src, dst, device):
        i = counter[0]
        counter[0] += 1
        copy = pltpu.make_async_remote_copy(
            src_ref=src,
            dst_ref=dst,
            send_sem=send_sem.at[i],
            recv_sem=recv_sem.at[i],
            device_id=device,
            device_id_type=MESH,
        )
        copy.start()
        sends.append(copy)
        return i

    def arrived(i, ref):
        pltpu.make_async_remote_copy(
            src_ref=ref,
            dst_ref=ref,
            send_sem=send_sem.at[i],
            recv_sem=recv_sem.at[i],
            device_id=core,
            device_id_type=MESH,
        ).wait_recv()

    barrier = pltpu.get_barrier_semaphore()
    partners = [lane(1), lane(3), lane(2), core, a_up, a_down, b_up, b_down]
    for partner in partners:
        pl.semaphore_signal(barrier, inc=1, device_id=partner, device_id_type=MESH)

    local = []

    def fetch(src, dst):
        copy = pltpu.make_async_copy(src, dst, local_sem.at[len(local)])
        copy.start()
        local.append(copy)

    for s in range(2):
        fetch(w_gate.at[s], wgu.at[0, :, pl.ds(s * 256, 128)])
        fetch(w_up.at[s], wgu.at[0, :, pl.ds(s * 256 + 128, 128)])
        fetch(w_down.at[s], wd.at[pl.ds(s * 128, 128), :])

    def attention(dt):
        rows = context[ds(((t + dt) % 4) * QR, QR), :]
        return jnp.dot(rows, w_out[...], preferred_element_type=F32)

    low, high = pl.ds(0, SR), pl.ds(SR, SR)
    att_send[0] = attention(2).astype(BF16)
    pl.semaphore_wait(barrier, len(partners))
    i_0 = send(att_send.at[0, low], att_half.at[0], lane(1))
    i_1 = send(att_send.at[0, high], att_half.at[1], lane(3))
    near = attention(1)
    att_send[1, high] = near[SR:].astype(BF16)
    other = attention(3)
    att_send[2, low] = other[:SR].astype(BF16)
    own = attention(0)
    sel = slot_choice(slot_expert[...], copy_pick[...])
    arrived(i_0, att_half.at[0])
    att_send[1, low] = (near[:SR] + att_half[0].astype(F32)).astype(BF16)
    i_0 = send(att_send.at[1], att_full.at[0], lane(1))
    arrived(i_1, att_half.at[1])
    att_send[2, high] = (other[SR:] + att_half[1].astype(F32)).astype(BF16)
    i_1 = send(att_send.at[2], att_full.at[1], lane(3))
    mid = resid[ds(t * QR, QR), :].astype(F32) + own
    ids = expert_ids[:, 0:QR]
    for q in range(1, 4):
        ids = jnp.where(t == q, expert_ids[:, q * QR : (q + 1) * QR], ids)
    expert = lax.broadcasted_iota(jnp.int32, (EXPERTS, QR), 0)
    named = ids[0:1] == expert
    for k in range(1, 8):
        named = named | (ids[k : k + 1] == expert)
    arrived(i_0, att_full.at[0])
    arrived(i_1, att_full.at[1])
    mid = mid + att_full[0].astype(F32) + att_full[1].astype(F32)
    middle[...] = mid
    square = jnp.mean(mid * mid, axis=-1, keepdims=True)
    normed = (mid * lax.rsqrt(square + EPSILON) * pre_gain[...].astype(F32)).astype(BF16)
    logits = lax.dot_general(
        w_router[...], normed, (((1,), (1,)), ((), ())), preferred_element_type=F32
    )
    raised = jnp.where(named, jnp.exp(jnp.where(named, logits, 0.0)), 0.0)
    weights = (raised / jnp.sum(raised, axis=0, keepdims=True)).astype(BF16)
    by_slot = lax.dot_general(
        weights, sel.astype(BF16), (((0,), (0,)), ((), ())), preferred_element_type=F32
    ).astype(BF16)

    def pos(da, db):
        return c * 16 + ((b + db) % 4) * 4 + (a + da) % 4

    def pos_core(da, db):
        return (1 - c) * 16 + ((a + db) % 4) * 4 + (b + da) % 4

    def group_own(q, db):
        return quarter[q] * 8 + c * 4 + (b + db) % 4

    def group_core(q, db):
        return quarter[q] * 8 + (1 - c) * 4 + (a + db) % 4

    def block(q, p):
        return xall.at[ds((quarter[q] * 32 + p) * QR, QR), :]

    def part(q, p, h):
        return xall.at[ds((quarter[q] * 32 + p) * QR + h * SR, SR), :]

    def part_of_lane(dt, p, h):
        return xall.at[ds(((((t + dt) % 4) // 2) * 32 + p) * QR + h * SR, SR), :]

    mine = pos(0, 0)
    rows = ds((quarter[0] * 32 + mine) * QR, QR)
    xall[rows, pl.ds(0, D)] = normed
    xall[rows, pl.ds(D, 128)] = jnp.concatenate(
        [by_slot, jnp.zeros((QR, 128 - SLOTS), BF16)], axis=1
    )

    i_a, i_ah, i_b, i_bp, i_c = {}, {}, {}, {}, {}

    def to_b(q, da):
        ref = block(q, pos(da, 0))
        i_b[q, da, 0] = send(ref, ref, b_up)
        i_b[q, da, 1] = send(ref, ref, b_down)
        i_c[q, da, 0] = send(ref, ref, core)

    def begin(q):
        ref = block(q, mine)
        i_a[q, 0] = send(ref, ref, a_up)
        i_a[q, 1] = send(ref, ref, a_down)
        to_b(q, 0)

    def near_a(q):
        for h, da, device in ((0, 3, a_up), (1, 1, a_down)):
            arrived(i_a[q, h], block(q, pos(da, 0)))
            ref = part(q, pos(da, 0), h)
            i_ah[q, h] = send(ref, ref, device)
            to_b(q, da)

    def far_a(q):
        for h in range(2):
            arrived(i_ah[q, h], part(q, pos(2, 0), h))
        to_b(q, 2)

    def near_b(q, da):
        for h, db, device in ((0, 3, b_up), (1, 1, b_down)):
            p = pos(da, db)
            arrived(i_b[q, da, h], block(q, p))
            ref = part(q, p, h)
            i_bp[q, da, h] = send(ref, ref, device)
            i_c[q, da, db] = send(block(q, p), block(q, p), core)

    def far_b(q, da):
        p = pos(da, 2)
        for h in range(2):
            arrived(i_bp[q, da, h], part(q, p, h))
        i_c[q, da, 2] = send(block(q, p), block(q, p), core)

    lanes = lax.broadcasted_iota(jnp.int32, (GROUP, 128), 1)

    def hidden_of(items):
        for q, db, which, _ in items:
            if which == "core" and (q, db) not in ready:
                ready.add((q, db))
                for da in (0, 3, 1, 2):
                    arrived(i_c[q, da, db], block(q, pos_core(da, db)))
        groups = [
            group_own(q, db) if which == "own" else group_core(q, db)
            for q, db, which, _ in items
        ]

        @pl.loop(0, len(items))
        def _(step):
            group, side = groups[0], items[0][3]
            for j in range(1, len(items)):
                group = jnp.where(step == j, groups[j], group)
                side = jnp.where(step == j, items[j][3], side)
            rows = ds(group * GROUP, GROUP)
            both = jnp.dot(
                xall[rows, pl.ds(0, D)], wgu[side], preferred_element_type=F32
            )
            by = xall[rows, pl.ds(D, 128)].astype(F32)
            for s in range(2):
                scale = jnp.sum(
                    jnp.where(lanes == ep * 2 + s, by, 0.0), axis=1, keepdims=True
                )
                gate = both[:, s * 256 : s * 256 + 128]
                upper = both[:, s * 256 + 128 : s * 256 + 256]
                value = gate / (1.0 + jnp.exp(-gate)) * upper * scale
                hid[rows, ds(side * 256 + s * 128, 128)] = value.astype(BF16)

    ready = set()

    begin(0)
    i_0 = send(part(0, mine, 0), relay.at[0], lane(1))
    i_1 = send(part(0, mine, 1), relay.at[1], lane(3))
    arrived(i_0, relay.at[0])
    i_0 = send(relay.at[0], part_of_lane(3, mine, 0), lane(1))
    arrived(i_1, relay.at[1])
    i_1 = send(relay.at[1], part_of_lane(1, mine, 1), lane(3))
    odd = t % 2
    neighbour = (lane(1 + 2 * odd), lane(3 - 2 * odd))
    i_w = []
    for w, at in ((w_gate, 0), (w_up, 128)):
        for s in range(2):
            ref = wgu.at[1, :, pl.ds(s * 256 + at, 128)]
            i_w.append((send(w.at[s], ref, neighbour[s]), ref))
    for s in range(2):
        ref = wd.at[pl.ds(256 + s * 128, 128), :]
        i_w.append((send(w_down.at[s], ref, neighbour[s]), ref))
    near_a(0)
    arrived(i_0, part(1, mine, 0))
    arrived(i_1, part(1, mine, 1))
    begin(1)
    near_b(0, 0)
    far_a(0)
    for copy in local:
        copy.wait()
    near_b(0, 3)
    near_a(1)
    near_b(0, 1)
    near_b(0, 2)
    near_b(1, 0)
    hidden_of([(0, 0, "own", 0), (0, 0, "core", 0)])
    far_a(1)
    far_b(0, 0)
    far_b(0, 3)
    near_b(1, 3)
    far_b(0, 1)
    near_b(1, 1)
    far_b(0, 2)
    near_b(1, 2)
    hidden_of([(0, db, w, 0) for db in (3, 1) for w in ("own", "core")])
    hidden_of([(q, db, w, 0) for q, db in ((0, 2), (1, 0)) for w in ("own", "core")])
    for i, ref in i_w[:4]:
        arrived(i, ref)
    far_b(1, 0)
    hidden_of([(0, db, w, 1) for db in (2, 0) for w in ("own", "core")])
    far_b(1, 3)
    hidden_of([(0, db, w, 1) for db in (3, 1) for w in ("own", "core")])
    far_b(1, 1)
    hidden_of(
        [(1, 0, w, 1) for w in ("own", "core")]
        + [(1, 3, w, side) for w in ("own", "core") for side in range(2)]
    )
    far_b(1, 2)

    order = (2, 1, 3, 0)
    i_y = {}

    def down(group, put):
        @pl.loop(0, 3)
        def _(step):
            columns = ds(step * 512, 512)
            put(
                columns,
                jnp.dot(
                    hid[ds(group * GROUP, GROUP), :],
                    wd[:, columns],
                    preferred_element_type=F32,
                ),
            )

    def for_core(q, k):
        def put(columns, value):
            yo[q, k, :, columns] = value.astype(BF16)

        down(group_core(q, order[k]), put)
        i_y[q, k] = send(yo.at[q, k], yr.at[q, k], core)

    def for_own(q, k):
        arrived(i_y[q, k], yr.at[q, k])

        def put(columns, value):
            ys[q, k, :, columns] = (value + yr[q, k, :, columns].astype(F32)).astype(BF16)

        down(group_own(q, order[k]), put)

    i_bh, i_bf, i_z = {}, {}, {}

    def rows_of(da, h=None):
        at = ((a + da) % 4) * QR
        return ds(at, QR) if h is None else ds(at + h * SR, SR)

    def far_sums(q):
        for da in order:
            for h, device in ((0, b_up), (1, b_down)):
                rows = rows_of(da, h)
                i_bh[q, da, h] = send(ys.at[q, 0, rows], bhalf.at[q, h, rows], device)

    def near_sums(q, k):
        h, device = k - 1, (b_up, b_down)[k - 1]
        for da in order:
            rows = rows_of(da, h)
            arrived(i_bh[q, da, h], bhalf.at[q, h, rows])
            ys[q, k, rows] = (
                ys[q, k, rows].astype(F32) + bhalf[q, h, rows].astype(F32)
            ).astype(BF16)
            rows = rows_of(da)
            i_bf[q, da, h] = send(ys.at[q, k, rows], bfull.at[q, h, rows], device)

    def last_sums(q):
        for j, da in enumerate(order):
            rows = rows_of(da)
            for h in range(2):
                arrived(i_bf[q, da, h], bfull.at[q, h, rows])
            total = (
                ys[q, 3, rows].astype(F32)
                + bfull[q, 0, rows].astype(F32)
                + bfull[q, 1, rows].astype(F32)
            )
            if j == 0:
                z[q, 0] = total.astype(BF16)
                i_z[0] = send(z.at[q, 0, low], ahalf.at[q, 0], a_up)
                i_z[1] = send(z.at[q, 0, high], ahalf.at[q, 1], a_down)
            elif j < 3:
                h, device = ((0, a_up), (1, a_down))[j - 1]
                arrived(i_z[h], ahalf.at[q, h])
                added = total[h * SR : (h + 1) * SR] + ahalf[q, h].astype(F32)
                kept = total[(1 - h) * SR : (2 - h) * SR]
                z[q, j, pl.ds(h * SR, SR)] = added.astype(BF16)
                z[q, j, pl.ds((1 - h) * SR, SR)] = kept.astype(BF16)
                i_z[2 + h] = send(z.at[q, j], afull.at[q, h], device)
            else:
                for h in range(2):
                    arrived(i_z[2 + h], afull.at[q, h])
                return total + afull[q, 0].astype(F32) + afull[q, 1].astype(F32)

    for i, ref in i_w[4:]:
        arrived(i, ref)
    for_core(0, 0)
    for_core(0, 1)
    for_own(0, 0)
    far_sums(0)
    hidden_of([(1, db, w, side) for db in (1, 2) for w in ("own", "core") for side in range(2)])
    for_core(1, 0)
    for_core(1, 1)
    for_own(1, 0)
    far_sums(1)
    for_own(1, 1)
    near_sums(1, 1)
    for_core(1, 2)
    for_core(0, 2)
    for_own(1, 2)
    near_sums(1, 2)
    for_own(0, 1)
    near_sums(0, 1)
    for_own(0, 2)
    near_sums(0, 2)
    for_core(1, 3)
    for_core(0, 3)
    for_own(1, 3)
    for_own(0, 3)
    psend[...] = last_sums(1).astype(BF16)
    i_0 = send(psend, precv, lane(2))
    mixture = last_sums(0)
    arrived(i_0, precv)
    value = middle[...] + (mixture + precv[...].astype(F32))
    square = jnp.mean(value * value, axis=-1, keepdims=True)
    value = value * lax.rsqrt(square + EPSILON) * final_gain[...].astype(F32)

    def out_rows(dt):
        return out.at[ds(((t + dt) % 4) * QR, QR), :]

    def out_half(dt, h):
        return out.at[ds(((t + dt) % 4) * QR + h * SR, SR), :]

    out[ds(t * QR, QR), :] = value.astype(BF16)
    i_0 = send(out_rows(0), out_rows(0), lane(1))
    i_1 = send(out_rows(0), out_rows(0), lane(3))
    arrived(i_0, out_rows(3))
    i_0 = send(out_half(3, 0), out_half(3, 0), lane(1))
    arrived(i_1, out_rows(1))
    i_1 = send(out_half(1, 1), out_half(1, 1), lane(3))
    arrived(i_0, out_half(2, 0))
    arrived(i_1, out_half(2, 1))
    for copy in sends:
        copy.wait_send()


COPIES = 160


def local(
    resid,
    context,
    w_out,
    pre_gain,
    final_gain,
    w_router,
    expert_ids,
    slot_expert,
    copy_pick,
    w_gate,
    w_up,
    w_down,
):
    vmem = pl.BlockSpec(memory_space=pltpu.VMEM)
    hbm = pl.BlockSpec(memory_space=pl.ANY)
    return pl.pallas_call(
        kernel,
        out_shape=jax.ShapeDtypeStruct((4 * QR, D), BF16),
        in_specs=[vmem] * 9 + [hbm] * 3,
        out_specs=vmem,
        scratch_shapes=[
            pltpu.VMEM((3, QR, D), BF16),
            pltpu.VMEM((2, SR, D), BF16),
            pltpu.VMEM((2, QR, D), BF16),
            pltpu.VMEM((QR, D), F32),
            pltpu.VMEM((2, SR, XW), BF16),
            pltpu.VMEM((16 * GROUP, XW), BF16),
            pltpu.VMEM((2, D, 512), BF16),
            pltpu.VMEM((512, D), BF16),
            pltpu.VMEM((16 * GROUP, 512), BF16),
            pltpu.VMEM((2, 4, GROUP, D), BF16),
            pltpu.VMEM((2, 4, GROUP, D), BF16),
            pltpu.VMEM((2, 4, GROUP, D), BF16),
            pltpu.VMEM((2, 2, GROUP, D), BF16),
            pltpu.VMEM((2, 2, GROUP, D), BF16),
            pltpu.VMEM((2, 3, QR, D), BF16),
            pltpu.VMEM((2, 2, SR, D), BF16),
            pltpu.VMEM((2, 2, QR, D), BF16),
            pltpu.VMEM((QR, D), BF16),
            pltpu.VMEM((QR, D), BF16),
            pltpu.SemaphoreType.DMA((COPIES,)),
            pltpu.SemaphoreType.DMA((COPIES,)),
            pltpu.SemaphoreType.DMA((6,)),
        ],
        compiler_params=pltpu.CompilerParams(
            collective_id=0, has_side_effects=True, vmem_limit_bytes=63 * 1024 * 1024
        ),
    )(
        resid,
        context,
        w_out,
        pre_gain,
        final_gain,
        w_router.T,
        expert_ids.T,
        slot_expert[None, :],
        copy_pick,
        w_gate,
        w_up,
        w_down,
    )


def solution(mesh):
    return jax.shard_map(
        local,
        mesh=mesh,
        in_specs=(
            P("ep", None),
            P("ep", "tp"),
            P("tp", None),
            P(),
            P(),
            P(),
            P("ep", None),
            P(),
            P("ep", None),
            P("ep", None, "tp"),
            P("ep", None, "tp"),
            P("ep", "tp", None),
        ),
        out_specs=P("ep", None),
        check_vma=False,
    )
```

time: 150 us -> 132 us (0.88)
  Pallas kernels: 141 us -> 130 us
  local copies, waits for them, and re-layouts: 7.93 us -> 2.06 us
    pallas_call x1, Pallas kernels: 141 us -> 130 us  [local(): pl.pallas_call(kernel, out_shape=jax.ShapeDtypeStruct((4 * QR, D), BF16),...]
    unnamed x3 -> x1, local copies, waits for them, and re-layouts: 5.36 us -> 2.06 us
    broadcast_in_dim x2 -> x0, local copies, waits for them, and re-layouts: 2.57 us -> none  [the longest x1 1.29 us: local(): final_gain[None, :]]
where the time goes in v2:
time: 132 us
  Pallas kernels  130 us (98%)
  local copies, waits for them, and re-layouts  2.06 us (2%)
    pallas_call x1, Pallas kernels, local(): pl.pallas_call(kernel, out_shape=jax.ShapeDtypeStruct((4 * QR, D), BF16),...  130 us

profile of v2, /device:TPU:0, one launch (start us, length us, event | category | flops | bytes accessed | tf_op | source)
XLA Modules:
  0.0 132.1 jit_solution(2126608573942032430)
XLA Ops:
  0.0 130.0 %shard_map.118 = bf16[256,1536]{1,0:T(8,128)(2,1)} custom-call(bf16[256,1536]{1,0:T(8,128)(2,1)} %resid.1, bf16[256,384]{1,0:T(8,128)(2,1)} %context.1, bf16[384,1536]{1,0:T(8,128)(2,1)} %w_out.1, bf16[1536]{0:T(1024)(128)(2,1)} %pre_gain.1, bf16[1536]{0:T(1024)(128)(2,1)} %final_gain.1, bf16[40,1536]{1,0:T(8,128)(2,1)} %bitcast.3, s32[8,256]{1,0:T(8,128)} %bitcast.4, ...), custom_call_target="tpu_custom_call" | custom-call | tf_op jit(solution)/shard_map/pallas_call | solution.py:504
  130.0 2.1 %copy.14 = bf16[256,1536]{1,0:T(8,128)(2,1)} copy(bf16[256,1536]{1,0:T(8,128)(2,1)} %shard_map.118) | data formatting | bytes 1572864
